TPU v7x, 32 devices: a whole 2x2x4 slice. The times are simulated.
32 devices in a mesh: groups: 2 (over y), row: 4 (over z), col: 4 (over x, core).
Axes of the slice: x: 2, y: 2, z: 4, core: 2. Of those that a mesh axis runs over, the one named last changes fastest.
Arguments:
- factor_blocks: bfloat16 [20, 4096, 4096], P('groups', 'row', 'col'), parts along dimension 0, may hold values from -0.0390625 to 0.0390625
- inverse_blocks: bfloat16 [10, 4096, 4096], P('groups', 'col', 'row'), parts along dimension 0, as said below
- right_sides: bfloat16 [10, 4096, 256], P('groups', 'row'), parts along dimension 0, may hold values from -6 to 6
Outputs:
- solution: bfloat16 [10, 4096, 256], P('groups', 'col', 'row'), parts along dimension 0
There are 2 independent parts, one for each index of `groups`. A program takes and returns all parts, laid end to end along the dimension named above; each array names one. Nothing has to cross between parts.
Inputs may be any that keep to these rules, and one draw needn't show every extreme that they name: `inverse_blocks`: each block is lower triangular with a diagonal of 0.5 to 2, hence invertible.
All inputs are finite; a program needn't handle non-finite values.
Results may differ from a plain program's by a relative error of at most 0.0095.
Values may be sent and summed in bfloat16 or wider, within the bound.
A program may use at most 64 MiB of HBM per device.

v0:
```python
import functools

import jax
import jax.numpy as jnp
from jax import lax
from jax.experimental import pallas as pl
from jax.experimental.pallas import tpu as pltpu
from jax.sharding import PartitionSpec as P

MESH = pl.DeviceIdType.MESH
CHAINS = 2
PIECES = 4
STAGGER = 1


def pair_index(block_row, column_index):
    return block_row * (block_row - 1) // 2 + column_index


def kernel(
    factor_hbm, inverse_hbm, right_hbm, solved,
    factor, inverse, right, partial, pair_out, pair_in, far_out, far_in, residual, line_out, line_in, cross_in,
    load_sem, col_send, col_recv, row_send, row_recv,
):
    f32, bf16 = jnp.float32, jnp.bfloat16
    steps, chains, col_rows, width = solved.shape
    rows = right.shape[1]
    half = rows // 2
    piece = col_rows // PIECES
    row_at = lax.axis_index("row")
    col_at = lax.axis_index("col")
    group_at = lax.axis_index("groups")
    core = lax.rem(col_at, 2)
    inner = jnp.logical_or(row_at == 1, row_at == 2)
    outer = jnp.logical_not(inner)
    owns = [row_at * chains // 4 == a for a in range(chains)]

    sibling = (group_at, row_at, col_at + 1 - 2 * core)
    far = (group_at, row_at, lax.rem(col_at + 2, 4))
    beside = (group_at, row_at + 1 - 2 * lax.rem(row_at, 2), col_at)
    across = (group_at, 3 - row_at, col_at)

    loads = {}
    order = [("r", i) for i in range(steps)][:1] + [("i", 0)]
    for i in range(1, steps):
        order += [("r", i)] + [("f", pair_index(i, j)) for j in range(i)] + [("i", i)]
    sources = {"f": (factor_hbm, factor), "i": (inverse_hbm, inverse), "r": (right_hbm, right)}
    for slot, (kind, at) in enumerate(order):
        src, dst = sources[kind]
        loads[kind, at] = pltpu.make_async_copy(src.at[at], dst.at[at], load_sem.at[slot])
        loads[kind, at].start()
    waited = set()

    def loaded(kind, at):
        if (kind, at) not in waited:
            waited.add((kind, at))
            loads[kind, at].wait()

    barrier = pltpu.get_barrier_semaphore()
    for peer in (sibling, far, beside):
        pl.semaphore_signal(barrier, inc=1, device_id=peer, device_id_type=MESH)

    @pl.when(inner)
    def _():
        pl.semaphore_signal(barrier, inc=1, device_id=across, device_id_type=MESH)
        pl.semaphore_wait(barrier, 4)

    @pl.when(outer)
    def _():
        pl.semaphore_wait(barrier, 3)

    def remote(src, dst, send, recv, peer):
        return pltpu.make_async_remote_copy(
            src_ref=src, dst_ref=dst, send_sem=send, recv_sem=recv, device_id=peer, device_id_type=MESH
        )

    mine = pl.ds(pl.multiple_of(core * half, half), half)
    other = pl.ds(pl.multiple_of((1 - core) * half, half), half)

    def dot(a, b):
        return jnp.dot(a, b, preferred_element_type=f32)

    def chain(a):
        lanes = slice(a * width, (a + 1) * width)
        for i in range(steps):
            if i > 0:
                to_pair = remote(pair_out.at[i - 1, a], pair_in.at[i - 1, a], col_send.at[i - 1, a, 0], col_recv.at[i - 1, a, 0], sibling)
                to_far = remote(far_out.at[i - 1, a], far_in.at[i - 1, a], col_send.at[i - 1, a, 1], col_recv.at[i - 1, a, 1], far)
                back = remote(residual.at[i, a, mine], residual.at[i, a, mine], col_send.at[i - 1, a, 2], col_recv.at[i - 1, a, 2], sibling)
                at = pair_index(i, i - 1)
                loaded("f", at)
                value = dot(factor[at, other, :], solved[i - 1, a])
                if i > 1:
                    value = value + partial[a, other, :]
                pair_out[i - 1, a] = value.astype(bf16)
                to_pair.start()
                value = dot(factor[at, mine, :], solved[i - 1, a])
                if i > 1:
                    value = value + partial[a, mine, :]
                partial[a, mine, :] = value
                yield
                to_pair.wait_recv()
                far_out[i - 1, a] = (partial[a, mine, :] + pair_in[i - 1, a].astype(f32)).astype(bf16)
                to_far.start()
                yield
                to_far.wait_recv()
                loaded("r", i)
                total = far_out[i - 1, a].astype(f32) + far_in[i - 1, a].astype(f32)
                residual[i, a, mine, :] = (right[i, mine, lanes].astype(f32) - total).astype(bf16)
                back.start()
                yield
                back.wait_recv()
            else:
                loaded("r", 0)
                residual[0, a] = right[0, :, lanes]
            loaded("i", i)
            final = i + 1 == steps
            takes = owns[a] if final else True
            gives = jnp.logical_not(owns[a]) if final else True
            spans = [pl.ds(k * piece, piece) for k in range(PIECES)]
            first = [remote(line_out.at[i, a, s], line_in.at[i, a, s], row_send.at[i, a, 0, k], row_recv.at[i, a, 0, k], beside) for k, s in enumerate(spans)]
            cross = [remote(line_out.at[i, a, s], cross_in.at[i, a, s], row_send.at[i, a, 1, k], row_recv.at[i, a, 1, k], across) for k, s in enumerate(spans)]
            last = [remote(solved.at[i, a, s], solved.at[i, a, s], row_send.at[i, a, 2, k], row_recv.at[i, a, 2, k], beside) for k, s in enumerate(spans)]
            for k, s in enumerate(spans):
                term = dot(inverse[i, s, :], residual[i, a])

                @pl.when(outer)
                def _():
                    line_out[i, a, s, :] = term.astype(bf16)
                    first[k].start()

                @pl.when(inner)
                def _():
                    first[k].wait_recv()
                    line_out[i, a, s, :] = (term + line_in[i, a, s, :].astype(f32)).astype(bf16)

                @pl.when(jnp.logical_and(inner, gives))
                def _():
                    cross[k].start()

            if i > 0 and i + 1 < steps:
                for j in range(i):
                    loaded("f", pair_index(i + 1, j))

                def ahead(t, carry):
                    tile = pl.ds(pl.multiple_of(t * piece, piece), piece)
                    value = dot(factor[pair_index(i + 1, 0), tile, :], solved[0, a])
                    for j in range(1, i):
                        value = value + dot(factor[pair_index(i + 1, j), tile, :], solved[j, a])
                    partial[a, tile, :] = value
                    return carry

                lax.fori_loop(0, rows // piece, ahead, 0)
            yield

            @pl.when(jnp.logical_and(inner, takes))
            def _():
                for k, s in enumerate(spans):
                    cross[k].wait_recv()
                    value = line_out[i, a, s, :].astype(f32) + cross_in[i, a, s, :].astype(f32)
                    solved[i, a, s, :] = value.astype(bf16)
                    last[k].start()

            yield

            @pl.when(jnp.logical_and(outer, takes))
            def _():
                for k in range(PIECES):
                    last[k].wait_recv()

            @pl.when(outer)
            def _():
                for k in range(PIECES):
                    first[k].wait_send()

            @pl.when(jnp.logical_and(inner, gives))
            def _():
                for k in range(PIECES):
                    cross[k].wait_send()

            @pl.when(jnp.logical_and(inner, takes))
            def _():
                for k in range(PIECES):
                    last[k].wait_send()

            if i > 0:
                to_pair.wait_send()
                to_far.wait_send()
                back.wait_send()

    running = [chain(a) for a in range(chains)]
    turn = 0
    while running:
        active = [g for a, g in enumerate(running) if a * STAGGER <= turn]
        for g in active:
            try:
                next(g)
            except StopIteration:
                running = [other_g for other_g in running if other_g is not g]
        turn += 1


def line_solve(factor_blocks, inverse_blocks, right_sides):
    steps, rows, angles = right_sides.shape
    pairs = factor_blocks.shape[0]
    col_rows = inverse_blocks.shape[1]
    width = angles // CHAINS
    half = rows // 2
    bf16 = jnp.bfloat16
    sweeps = steps - 1
    wide = (steps, CHAINS, col_rows, width)
    dma = pltpu.SemaphoreType.DMA
    solved = pl.pallas_call(
        kernel,
        out_shape=jax.ShapeDtypeStruct(wide, bf16),
        in_specs=[pl.BlockSpec(memory_space=pl.ANY)] * 3,
        out_specs=pl.BlockSpec(memory_space=pltpu.VMEM),
        scratch_shapes=[
            pltpu.VMEM(factor_blocks.shape, bf16),
            pltpu.VMEM(inverse_blocks.shape, bf16),
            pltpu.VMEM(right_sides.shape, bf16),
            pltpu.VMEM((CHAINS, rows, width), jnp.float32),
            pltpu.VMEM((sweeps, CHAINS, half, width), bf16),
            pltpu.VMEM((sweeps, CHAINS, half, width), bf16),
            pltpu.VMEM((sweeps, CHAINS, half, width), bf16),
            pltpu.VMEM((sweeps, CHAINS, half, width), bf16),
            pltpu.VMEM((steps, CHAINS, rows, width), bf16),
            pltpu.VMEM(wide, bf16),
            pltpu.VMEM(wide, bf16),
            pltpu.VMEM(wide, bf16),
            dma((pairs + 2 * steps,)),
            dma((sweeps, CHAINS, 3)),
            dma((sweeps, CHAINS, 3)),
            dma((steps, CHAINS, 3, PIECES)),
            dma((steps, CHAINS, 3, PIECES)),
        ],
        compiler_params=pltpu.CompilerParams(
            collective_id=0, has_side_effects=True, vmem_limit_bytes=67043328
        ),
    )(factor_blocks, inverse_blocks, right_sides)
    share = angles // lax.axis_size("row")
    start = lax.axis_index("row") * share
    held = lax.dynamic_index_in_dim(solved, start // width, axis=1, keepdims=False)
    return lax.dynamic_slice_in_dim(held, lax.rem(start, width), share, axis=2)


def plain_solve(factor_blocks, inverse_blocks, right_sides):
    steps_total = right_sides.shape[0]
    solved = []
    outputs = []
    for block_row in range(steps_total):
        residual = right_sides[block_row].astype(jnp.float32)
        if block_row > 0:
            partial_value = jnp.zeros(residual.shape, jnp.float32)
            for column_index in range(block_row):
                partial_value = partial_value + jnp.dot(
                    factor_blocks[pair_index(block_row, column_index)],
                    solved[column_index],
                    preferred_element_type=jnp.float32,
                )
            residual = residual - lax.psum(partial_value, "col")
        residual_bf = residual.astype(jnp.bfloat16)
        term = jnp.dot(inverse_blocks[block_row], residual_bf, preferred_element_type=jnp.float32)
        share = lax.psum_scatter(term, "row", scatter_dimension=1, tiled=True).astype(jnp.bfloat16)
        outputs.append(share)
        if block_row + 1 < steps_total:
            solved.append(lax.all_gather(share, "row", axis=1, tiled=True))
    return jnp.stack(outputs, axis=0)


def solution(mesh):
    placed = (P("groups", "row", "col"), P("groups", "col", "row"), P("groups", "row", None))
    per_device = line_solve if mesh.shape["row"] == 4 and mesh.shape["col"] == 4 else plain_solve
    return jax.shard_map(
        per_device, mesh=mesh, in_specs=placed, out_specs=P("groups", "col", "row"), check_vma=False
    )
```

profile of v0, /device:TPU:26, one launch (start us, length us, event | category | flops | bytes accessed | tf_op | source)
XLA Modules:
  0.0 136.3 jit_solution(8197540777103053289)
XLA Ops:
  0.0 133.3 %shard_map.37 = bf16[5,2,1024,128]{3,2,1,0:T(8,128)(2,1)} custom-call(bf16[10,1024,1024]{2,1,0:T(8,128)(2,1)} %factor_hbm.1, bf16[5,1024,1024]{2,1,0:T(8,128)(2,1)} %inverse_hbm.1, bf16[5,1024,256]{2,1,0:T(8,128)(2,1)} %right_hbm.1), custom_call_target="tpu_custom_call" | custom-call | tf_op jit(solution)/shard_map/pallas_call | solution.py:213
  133.3 1.7 %constant_dynamic-slice_fusion = bf16[5,1,1024,64]{3,2,1,0:T(8,128)(2,1)S(1)} fusion(bf16[5,2,1024,128]{3,2,1,0:T(8,128)(2,1)} %shard_map.37, s32[]{:T(128)S(6)} %select_n.18, s32[]{:T(128)S(6)} %select_n.20), kind=kLoop, calls=%fused_computation | loop fusion | bytes 1310728 | tf_op jit(solution)/shard_map/dynamic_slice | solution.py:244
  135.0 1.3 copy.4
where the time goes:
time: 136 us
  Pallas kernels  133 us (98%)
  local copies, waits for them, and re-layouts  3.04 us (2%)
    pallas_call x1, Pallas kernels, line_solve(): pl.pallas_call(kernel, out_shape=jax.ShapeDtypeStruct(wide, bf16), in_spe...  133 us
    dynamic_slice x2, local copies, waits for them, and re-layouts, line_solve(): return lax.dynamic_slice_in_dim(held, lax.rem(start, width), share, axis=2)  3.04 us

commit v1 on v0

v1 whole, which is shorter than its diff:
```python
import jax
import jax.numpy as jnp
from jax import lax
from jax.experimental import pallas as pl
from jax.experimental.pallas import tpu as pltpu
from jax.sharding import PartitionSpec as P

MESH = pl.DeviceIdType.MESH
CHAINS = 2
PIECES = 4
INVERSE_SLOTS = 3
f32, bf16 = jnp.float32, jnp.bfloat16


def pair_index(block_row, column_index):
    return block_row * (block_row - 1) // 2 + column_index


def dot_t(a, b):
    return lax.dot_general(a, b, (((1,), (1,)), ((), ())), preferred_element_type=f32)


def kernel(
    factor_hbm, inverse_hbm, right_hbm, solved,
    factor, inverse, right, turned, x, in_right, in_left, out, term, partial, ahead, far_out, far_in, residual,
    load_sem, push_send, push_recv, far_send, far_recv, line_send, line_recv, give_send, give_recv, credit,
):
    steps, _, width, piece = solved.shape
    pairs = factor_hbm.shape[0]
    rows = right.shape[1]
    factor_slots = factor.shape[0]
    row = lax.axis_index("row")
    col = lax.axis_index("col")
    group = lax.axis_index("groups")
    core = lax.rem(col, 2)
    side = col // 2
    sibling = (group, row, col + 1 - 2 * core)
    far = (group, row, lax.rem(col + 2, 4))
    left = (group, jnp.maximum(row - 1, 0), col)
    right_dev = (group, jnp.minimum(row + 1, 3), col)
    last = steps - 1

    def remote(src, dst, send, recv, peer):
        return pltpu.make_async_remote_copy(
            src_ref=src, dst_ref=dst, send_sem=send, recv_sem=recv, device_id=peer, device_id_type=MESH
        )

    def local_tile(kind, at):
        if kind == "f":
            return pltpu.make_async_copy(factor_hbm.at[at], factor.at[at % factor_slots, core], load_sem.at[at])
        return pltpu.make_async_copy(inverse_hbm.at[at], inverse.at[at % INVERSE_SLOTS, core], load_sem.at[pairs + at])

    def pushed_tile(kind, at):
        if kind == "f":
            dst = factor.at[at % factor_slots, core]
            return remote(factor_hbm.at[at], dst, push_send.at[at], push_recv.at[at], sibling)
        dst = inverse.at[at % INVERSE_SLOTS, core]
        return remote(inverse_hbm.at[at], dst, push_send.at[pairs + at], push_recv.at[pairs + at], sibling)

    def landed_tile(kind, at):
        if kind == "f":
            dst = factor.at[at % factor_slots, 1 - core]
            return remote(factor_hbm.at[at], dst, push_send.at[at], push_recv.at[at], sibling)
        dst = inverse.at[at % INVERSE_SLOTS, 1 - core]
        return remote(inverse_hbm.at[at], dst, push_send.at[pairs + at], push_recv.at[pairs + at], sibling)

    tiles = [("i", 0)]
    for i in range(1, steps):
        tiles += [("f", pair_index(i, j)) for j in range(i)] + [("i", i)]
    fresh = [t for t in tiles if not (t[0] == "f" and t[1] >= factor_slots or t[0] == "i" and t[1] >= INVERSE_SLOTS)]
    early = [t for t in fresh if t[0] == "i" or t[1] < pair_index(4, 0)]
    late = [t for t in fresh if t not in early]
    ready = set()

    def loaded(kind, at):
        if (kind, at) not in ready:
            ready.add((kind, at))
            local_tile(kind, at).wait()
            landed_tile(kind, at).wait_recv()

    lanes = pl.ds(pl.multiple_of(core * CHAINS * width, CHAINS * width), CHAINS * width)

    def right_load(i):
        return pltpu.make_async_copy(right_hbm.at[i, :, lanes], right.at[i], load_sem.at[pairs + steps + i])

    right_load(0).start()
    for kind, at in fresh[:1]:
        local_tile(kind, at).start()
    for i in range(1, steps):
        right_load(i).start()
    for kind, at in fresh[1:]:
        local_tile(kind, at).start()

    barrier = pltpu.get_barrier_semaphore()
    for peer in (sibling, far):
        pl.semaphore_signal(barrier, inc=1, device_id=peer, device_id_type=MESH)

    @pl.when(row > 0)
    def _():
        pl.semaphore_signal(barrier, inc=1, device_id=left, device_id_type=MESH)

    @pl.when(row < 3)
    def _():
        pl.semaphore_signal(barrier, inc=1, device_id=right_dev, device_id_type=MESH)

    @pl.when(jnp.logical_or(row == 0, row == 3))
    def _():
        pl.semaphore_wait(barrier, 3)

    @pl.when(jnp.logical_and(row > 0, row < 3))
    def _():
        pl.semaphore_wait(barrier, 4)

    for kind, at in early:
        pushed_tile(kind, at).start()

    def turn(i):
        right_load(i).wait()
        turned[i] = right[i].T

    def going_right(i, k, p, src, dst):
        return remote(src, dst, line_send.at[i, k, 0, p], line_recv.at[i, k, 0, p], right_dev)

    def going_left(i, k, p, src, dst):
        return remote(src, dst, line_send.at[i, k, 1, p], line_recv.at[i, k, 1, p], left)

    def each(body, start=0):
        def step(p, carry):
            body(p, 2 * side + p // 2)
            return carry

        lax.fori_loop(start, PIECES, step, 0)

    def span(p):
        return pl.ds(pl.multiple_of(lax.rem(p, 2) * piece, piece), piece)

    def solve(i, k):
        chain = slice(k * width, (k + 1) * width)
        if i == 0:
            residual[k] = turned[0, chain, :]
        else:
            for h in range(2):
                cols = slice(h * (rows // 2), (h + 1) * (rows // 2))
                far_copy(i, k, h).wait_recv()
                total = partial[k, :, cols] + far_in[i - 1, k, h].astype(f32)
                residual[k, :, cols] = (turned[i, chain, cols].astype(f32) - total).astype(bf16)
        loaded("i", i)
        par = i % 2
        goal = 2 * core + k

        def body(p, c):
            @pl.when(c >= row)
            def _():
                value = dot_t(residual[k], inverse[i % INVERSE_SLOTS, p // 2, span(p), :])
                term[k, p] = value
                out[par, k, p] = value.astype(bf16)
                if i < last:
                    @pl.when(jnp.logical_and(row == 0, c == 0))
                    def _():
                        x[i, k, p] = value.astype(bf16)
                        going_right(i, k, p, x.at[i, k, p], x.at[i, k, p]).start()

                    @pl.when(jnp.logical_and(row == 0, c > 0))
                    def _():
                        going_right(i, k, p, out.at[par, k, p], in_right.at[par, k, p]).start()

                    @pl.when(jnp.logical_and(row >= 2, c == row))
                    def _():
                        going_left(i, k, p, out.at[par, k, p], in_left.at[par, k, p]).start()
                else:
                    @pl.when(jnp.logical_and(row == 0, goal > 0))
                    def _():
                        going_right(i, k, p, out.at[par, k, p], in_right.at[par, k, p]).start()

                    @pl.when(jnp.logical_and(row > goal, c == row))
                    def _():
                        going_left(i, k, p, out.at[par, k, p], in_left.at[par, k, p]).start()

        each(body)

    def came_right(i, k, p):
        going_right(i, k, p, out.at[0, k, p], in_right.at[0, k, p]).wait_recv()

    def came_left(i, k, p):
        going_left(i, k, p, out.at[0, k, p], in_left.at[0, k, p]).wait_recv()

    def relay_first(i, k):
        par = i % 2

        @pl.when(row == 1)
        def _():
            def body(p, c):
                came_right(i, k, p)

                @pl.when(c == 0)
                def _():
                    going_right(i, k, p, x.at[i, k, p], x.at[i, k, p]).start()

                @pl.when(c == 1)
                def _():
                    x[i, k, p] = (in_right[par, k, p].astype(f32) + term[k, p]).astype(bf16)
                    going_right(i, k, p, x.at[i, k, p], x.at[i, k, p]).start()
                    going_left(i, k, p, x.at[i, k, p], x.at[i, k, p]).start()

                @pl.when(c >= 2)
                def _():
                    out[par, k, p] = (in_right[par, k, p].astype(f32) + term[k, p]).astype(bf16)
                    going_right(i, k, p, out.at[par, k, p], in_right.at[par, k, p]).start()

            each(body)

        @pl.when(jnp.logical_and(row == 2, side == 1))
        def _():
            def body(p, c):
                came_left(i, k, p)
                out[par, k, p] = (in_left[par, k, p].astype(f32) + term[k, p]).astype(bf16)
                going_left(i, k, p, out.at[par, k, p], in_left.at[par, k, p]).start()

            each(body, PIECES // 2)

    def relay_second(i, k):
        par = i % 2

        @pl.when(jnp.logical_and(row == 1, side == 1))
        def _():
            def body(p, c):
                came_left(i, k, p)
                x[i, k, p] = (out[par, k, p].astype(f32) + in_left[par, k, p].astype(f32)).astype(bf16)
                going_left(i, k, p, x.at[i, k, p], x.at[i, k, p]).start()

            each(body)

        @pl.when(row == 2)
        def _():
            def body(p, c):
                came_right(i, k, p)

                @pl.when(c >= 2)
                def _():
                    x[i, k, p] = (out[par, k, p].astype(f32) + in_right[par, k, p].astype(f32)).astype(bf16)

                going_right(i, k, p, x.at[i, k, p], x.at[i, k, p]).start()

            each(body)

    def came_last(i, k, p, c):
        @pl.when(jnp.logical_and(row == 0, c >= 1))
        def _():
            came_left(i, k, p)

        @pl.when(row == 3)
        def _():
            came_right(i, k, p)

    def sent(i, k):
        goal = 2 * core + k
        to_right = row < 3 if i < last else row < goal
        to_left = row > 0 if i < last else row > goal

        def body(p, c):
            @pl.when(to_right)
            def _():
                going_right(i, k, p, out.at[0, k, p], in_right.at[0, k, p]).wait_send()

            @pl.when(jnp.logical_and(to_left, c >= row))
            def _():
                going_left(i, k, p, out.at[0, k, p], in_left.at[0, k, p]).wait_send()

        each(body)

    def collect(i, k):
        par = i % 2
        goal = 2 * core + k

        @pl.when(jnp.logical_and(row < goal, row >= 1))
        def _():
            def body(p, c):
                came_right(i, k, p)

                @pl.when(c >= row)
                def _():
                    out[par, k, p] = (in_right[par, k, p].astype(f32) + term[k, p]).astype(bf16)
                    going_right(i, k, p, out.at[par, k, p], in_right.at[par, k, p]).start()

                @pl.when(c < row)
                def _():
                    going_right(i, k, p, in_right.at[par, k, p], in_right.at[par, k, p]).start()

            each(body)

        @pl.when(row > goal)
        def _():
            def body(p, c):
                @pl.when(c > row)
                def _():
                    came_left(i, k, p)
                    out[par, k, p] = (in_left[par, k, p].astype(f32) + term[k, p]).astype(bf16)
                    going_left(i, k, p, out.at[par, k, p], in_left.at[par, k, p]).start()

            each(body)

    def keep(i, k):
        par = i % 2
        goal = 2 * core + k

        @pl.when(row == goal)
        def _():
            def body(p, c):
                @pl.when(row >= 1)
                def _():
                    came_right(i, k, p)

                @pl.when(c > row)
                def _():
                    came_left(i, k, p)

                @pl.when(c < row)
                def _():
                    x[i, k, p] = in_right[par, k, p]

                @pl.when(c >= row)
                def _():
                    @pl.when(row >= 1)
                    def _():
                        term[k, p] = term[k, p] + in_right[par, k, p].astype(f32)

                    @pl.when(c > row)
                    def _():
                        term[k, p] = term[k, p] + in_left[par, k, p].astype(f32)

                    x[i, k, p] = term[k, p].astype(bf16)

            each(body)

    def far_copy(i, k, h):
        return remote(far_out.at[i - 1, k, h], far_in.at[i - 1, k, h], far_send.at[i - 1, k, h], far_recv.at[i - 1, k, h], far)

    def update(i, k):
        at = pair_index(i, i - 1)
        loaded("f", at)
        if i > 1:
            partial[k] = ahead[k * width : (k + 1) * width, :]
        else:
            partial[k] = jnp.zeros_like(partial[k])

        def body(p, c):
            came_last(i - 1, k, p, c)
            partial[k] += dot_t(x[i - 1, k, p], factor[at % factor_slots, p // 2, :, span(p)])

        each(body)
        for h in range(2):
            far_out[i - 1, k, h] = partial[k, :, h * (rows // 2) : (h + 1) * (rows // 2)].astype(bf16)
            far_copy(i, k, h).start()
        sent(i - 1, k)

    def look_ahead(i):
        for j in range(i - 1):
            at = pair_index(i, j)
            loaded("f", at)

            def body(p, c):
                value = dot_t(x[j, :, p].reshape(CHAINS * width, piece), factor[at % factor_slots, p // 2, :, span(p)])
                if j == 0:
                    @pl.when(p == 0)
                    def _():
                        ahead[...] = value

                    @pl.when(p > 0)
                    def _():
                        ahead[...] += value
                else:
                    ahead[...] += value

            each(body)

    owner = core == row // 2
    chain_at = lax.rem(row, 2)

    def give_copy(i, h):
        return remote(x.at[i, chain_at, 2 * (1 - core) + h], solved.at[i, h], give_send.at[i, h], give_recv.at[i, h], sibling)

    def give(i):
        @pl.when(owner)
        def _():
            for h in range(2):
                give_copy(i, h).start()
            for h in range(2):
                solved[i, h] = x[i, chain_at, 2 * core + h]

    def allow(n):
        pl.semaphore_signal(credit.at[n], inc=1, device_id=sibling, device_id_type=MESH)

    def refill(n, kind, at):
        pl.semaphore_wait(credit.at[n], 1)
        local_tile(kind, at).start()
        pushed_tile(kind, at).start()

    a, b = 0, 1
    turn(0)
    solve(0, a)
    solve(0, b)
    allow(0)
    turn(1)
    relay_first(0, a)
    relay_second(0, a)
    update(1, a)
    refill(0, "i", 3)
    for kind, at in late:
        pushed_tile(kind, at).start()
    relay_first(0, b)
    relay_second(0, b)
    for i in range(1, steps):
        solve(i, a)
        update(i, b)
        give(i - 1)
        if i == 1:
            allow(1)
        if i < last:
            relay_first(i, a)
            relay_second(i, a)
            solve(i, b)
            if i == 1:
                allow(2)
            turn(i + 1)
            look_ahead(i + 1)
            update(i + 1, a)
            if i == 1:
                refill(1, "f", factor_slots)
                refill(2, "i", 4)
            relay_first(i, b)
            relay_second(i, b)
        else:
            collect(i, a)
            solve(i, b)
            collect(i, b)
            keep(i, a)
            keep(i, b)
            give(i)
            sent(i, a)
            sent(i, b)

    @pl.when(owner)
    def _():
        for i in range(steps):
            for h in range(2):
                give_copy(i, h).wait_send()

    @pl.when(jnp.logical_not(owner))
    def _():
        for i in range(steps):
            for h in range(2):
                give_copy(i, h).wait_recv()

    for i in range(1, steps):
        for k in range(CHAINS):
            for h in range(2):
                far_copy(i, k, h).wait_send()
    for kind, at in tiles:
        pushed_tile(kind, at).wait_send()


def line_solve(factor_blocks, inverse_blocks, right_sides):
    steps, rows, angles = right_sides.shape
    pairs = factor_blocks.shape[0]
    col_rows = inverse_blocks.shape[1]
    width = angles // lax.axis_size("row")
    both = CHAINS * width
    half = rows // 2
    piece = col_rows // 2
    line = (2, CHAINS, PIECES, width, piece)
    dma = pltpu.SemaphoreType.DMA
    solved = pl.pallas_call(
        kernel,
        out_shape=jax.ShapeDtypeStruct((steps, 2, width, piece), bf16),
        in_specs=[pl.BlockSpec(memory_space=pl.ANY)] * 3,
        out_specs=pl.BlockSpec(memory_space=pltpu.VMEM),
        scratch_shapes=[
            pltpu.VMEM((pairs - 1, 2) + factor_blocks.shape[1:], bf16),
            pltpu.VMEM((INVERSE_SLOTS, 2) + inverse_blocks.shape[1:], bf16),
            pltpu.VMEM((steps, rows, both), bf16),
            pltpu.VMEM((steps, both, rows), bf16),
            pltpu.VMEM((steps, CHAINS, PIECES, width, piece), bf16),
            pltpu.VMEM(line, bf16),
            pltpu.VMEM(line, bf16),
            pltpu.VMEM(line, bf16),
            pltpu.VMEM((CHAINS, PIECES, width, piece), f32),
            pltpu.VMEM((CHAINS, width, rows), f32),
            pltpu.VMEM((both, rows), f32),
            pltpu.VMEM((steps - 1, CHAINS, 2, width, half), bf16),
            pltpu.VMEM((steps - 1, CHAINS, 2, width, half), bf16),
            pltpu.VMEM((CHAINS, width, rows), bf16),
            dma((pairs + 2 * steps,)),
            dma((pairs + steps,)),
            dma((pairs + steps,)),
            dma((steps - 1, CHAINS, 2)),
            dma((steps - 1, CHAINS, 2)),
            dma((steps, CHAINS, 2, PIECES)),
            dma((steps, CHAINS, 2, PIECES)),
            dma((steps, 2)),
            dma((steps, 2)),
            pltpu.SemaphoreType.REGULAR((3,)),
        ],
        compiler_params=pltpu.CompilerParams(
            collective_id=0, has_side_effects=True, vmem_limit_bytes=67043328
        ),
    )(factor_blocks, inverse_blocks, right_sides)
    return solved.transpose(0, 1, 3, 2).reshape(steps, col_rows, width)


def plain_solve(factor_blocks, inverse_blocks, right_sides):
    steps_total = right_sides.shape[0]
    solved = []
    outputs = []
    for block_row in range(steps_total):
        residual = right_sides[block_row].astype(jnp.float32)
        if block_row > 0:
            partial_value = jnp.zeros(residual.shape, jnp.float32)
            for column_index in range(block_row):
                partial_value = partial_value + jnp.dot(
                    factor_blocks[pair_index(block_row, column_index)],
                    solved[column_index],
                    preferred_element_type=jnp.float32,
                )
            residual = residual - lax.psum(partial_value, "col")
        residual_bf = residual.astype(jnp.bfloat16)
        term = jnp.dot(inverse_blocks[block_row], residual_bf, preferred_element_type=jnp.float32)
        share = lax.psum_scatter(term, "row", scatter_dimension=1, tiled=True).astype(jnp.bfloat16)
        outputs.append(share)
        if block_row + 1 < steps_total:
            solved.append(lax.all_gather(share, "row", axis=1, tiled=True))
    return jnp.stack(outputs, axis=0)


def solution(mesh):
    placed = (P("groups", "row", "col"), P("groups", "col", "row"), P("groups", "row", None))
    per_device = line_solve if mesh.shape["row"] == 4 and mesh.shape["col"] == 4 else plain_solve
    return jax.shard_map(
        per_device, mesh=mesh, in_specs=placed, out_specs=P("groups", "col", "row"), check_vma=False
    )
```

time: 136 us -> 113 us (0.83)
  the two profiles are of different devices: /device:TPU:26 before, /device:TPU:2 now
where the time goes in v1:
time: 113 us
  Pallas kernels  111 us (98%)
  local copies, waits for them, and re-layouts  2.01 us (2%)
    pallas_call x1, Pallas kernels, line_solve(): pl.pallas_call(kernel, out_shape=jax.ShapeDtypeStruct((steps, 2, width, p...  111 us

profile of v1, /device:TPU:2, one launch (start us, length us, event | category | flops | bytes accessed | tf_op | source)
XLA Modules:
  0.0 112.8 jit_solution(8623316085241680047)
XLA Ops:
  0.0 110.8 %shard_map.37 = bf16[5,2,64,512]{3,2,1,0:T(8,128)(2,1)} custom-call(bf16[10,1024,1024]{2,1,0:T(8,128)(2,1)} %factor_hbm.1, bf16[5,1024,1024]{2,1,0:T(8,128)(2,1)} %inverse_hbm.1, bf16[5,1024,256]{2,1,0:T(8,128)(2,1)} %right_hbm.1), custom_call_target="tpu_custom_call" | custom-call | tf_op jit(solution)/shard_map/pallas_call | solution.py:472
  110.8 2.0 %copy.5 = bf16[5,2,8,8,512]{4,3,1,2,0:T(8,128)(2,1)} copy(bf16[5,2,8,8,512]{4,3,2,1,0:T(8,128)(2,1)} %bitcast.3) | data formatting | bytes 1310720 | tf_op jit(solution)/shard_map/reshape | solution.py:507

commit v2 on v1

--- a/solution.py
+++ b/solution.py
@@ -9,6 +9,7 @@
 CHAINS = 2
 PIECES = 4
 INVERSE_SLOTS = 3
+MORE = 6
 f32, bf16 = jnp.float32, jnp.bfloat16
 
 
@@ -23,9 +24,10 @@
 def kernel(
     factor_hbm, inverse_hbm, right_hbm, solved,
     factor, inverse, right, turned, x, in_right, in_left, out, term, partial, ahead, far_out, far_in, residual,
-    load_sem, push_send, push_recv, far_send, far_recv, line_send, line_recv, give_send, give_recv, credit,
+    load_sem, push_send, push_recv, far_send, far_recv, line_send, line_recv, give_send, give_recv, keep_sem, first_sem, credit,
 ):
-    steps, _, width, piece = solved.shape
+    steps, width = solved.shape[:2]
+    piece = x.shape[4]
     pairs = factor_hbm.shape[0]
     rows = right.shape[1]
     factor_slots = factor.shape[0]
@@ -45,6 +47,9 @@
             src_ref=src, dst_ref=dst, send_sem=send, recv_sem=recv, device_id=peer, device_id_type=MESH
         )
 
+    def span(p):
+        return pl.ds(pl.multiple_of(lax.rem(p, 2) * piece, piece), piece)
+
     def local_tile(kind, at):
         if kind == "f":
             return pltpu.make_async_copy(factor_hbm.at[at], factor.at[at % factor_slots, core], load_sem.at[at])
@@ -70,7 +75,7 @@
     fresh = [t for t in tiles if not (t[0] == "f" and t[1] >= factor_slots or t[0] == "i" and t[1] >= INVERSE_SLOTS)]
     early = [t for t in fresh if t[0] == "i" or t[1] < pair_index(4, 0)]
     late = [t for t in fresh if t not in early]
-    ready = set()
+    ready = {tiles[0]}
 
     def loaded(kind, at):
         if (kind, at) not in ready:
@@ -83,9 +88,15 @@
     def right_load(i):
         return pltpu.make_async_copy(right_hbm.at[i, :, lanes], right.at[i], load_sem.at[pairs + steps + i])
 
+    def first_load(h):
+        return pltpu.make_async_copy(inverse_hbm.at[0, span(h)], inverse.at[0, core, span(h)], first_sem.at[0, h])
+
+    def first_push(h, par):
+        return remote(inverse_hbm.at[0, span(h)], inverse.at[0, par, span(h)], first_sem.at[1, h], first_sem.at[2, h], sibling)
+
     right_load(0).start()
-    for kind, at in fresh[:1]:
-        local_tile(kind, at).start()
+    for h in range(2):
+        first_load(h).start()
     for i in range(1, steps):
         right_load(i).start()
     for kind, at in fresh[1:]:
@@ -111,7 +122,9 @@
     def _():
         pl.semaphore_wait(barrier, 4)
 
-    for kind, at in early:
+    for h in range(2):
+        first_push(h, core).start()
+    for kind, at in early[1:]:
         pushed_tile(kind, at).start()
 
     def turn(i):
@@ -124,15 +137,18 @@
     def going_left(i, k, p, src, dst):
         return remote(src, dst, line_send.at[i, k, 1, p], line_recv.at[i, k, 1, p], left)
 
-    def each(body, start=0):
+    def each(body, start=0, turned_by=0):
         def step(p, carry):
+            p = lax.rem(p + turned_by, PIECES)
             body(p, 2 * side + p // 2)
             return carry
 
         lax.fori_loop(start, PIECES, step, 0)
 
-    def span(p):
-        return pl.ds(pl.multiple_of(lax.rem(p, 2) * piece, piece), piece)
+    def order(i):
+        if i == 0:
+            return 2 * core
+        return 2 * (1 - core) if i == last else 0
 
     def solve(i, k):
         chain = slice(k * width, (k + 1) * width)
@@ -147,8 +163,19 @@
         loaded("i", i)
         par = i % 2
         goal = 2 * core + k
+        if i >= 2:
+            sent(i - 2, k)
 
         def body(p, c):
+            if i == 0 and k == 0:
+                @pl.when(p // 2 == core)
+                def _():
+                    first_load(lax.rem(p, 2)).wait()
+
+                @pl.when(p // 2 != core)
+                def _():
+                    first_push(lax.rem(p, 2), 1 - core).wait_recv()
+
             @pl.when(c >= row)
             def _():
                 value = dot_t(residual[k], inverse[i % INVERSE_SLOTS, p // 2, span(p), :])
@@ -176,7 +203,7 @@
                     def _():
                         going_left(i, k, p, out.at[par, k, p], in_left.at[par, k, p]).start()
 
-        each(body)
+        each(body, 0, order(i))
 
     def came_right(i, k, p):
         going_right(i, k, p, out.at[0, k, p], in_right.at[0, k, p]).wait_recv()
@@ -184,64 +211,52 @@
     def came_left(i, k, p):
         going_left(i, k, p, out.at[0, k, p], in_left.at[0, k, p]).wait_recv()
 
-    def relay_first(i, k):
+    def relay_first(i, k, p, c):
         par = i % 2
 
         @pl.when(row == 1)
         def _():
-            def body(p, c):
-                came_right(i, k, p)
-
-                @pl.when(c == 0)
-                def _():
-                    going_right(i, k, p, x.at[i, k, p], x.at[i, k, p]).start()
-
-                @pl.when(c == 1)
-                def _():
-                    x[i, k, p] = (in_right[par, k, p].astype(f32) + term[k, p]).astype(bf16)
-                    going_right(i, k, p, x.at[i, k, p], x.at[i, k, p]).start()
-                    going_left(i, k, p, x.at[i, k, p], x.at[i, k, p]).start()
-
-                @pl.when(c >= 2)
-                def _():
-                    out[par, k, p] = (in_right[par, k, p].astype(f32) + term[k, p]).astype(bf16)
-                    going_right(i, k, p, out.at[par, k, p], in_right.at[par, k, p]).start()
-
-            each(body)
-
-        @pl.when(jnp.logical_and(row == 2, side == 1))
-        def _():
-            def body(p, c):
-                came_left(i, k, p)
-                out[par, k, p] = (in_left[par, k, p].astype(f32) + term[k, p]).astype(bf16)
-                going_left(i, k, p, out.at[par, k, p], in_left.at[par, k, p]).start()
-
-            each(body, PIECES // 2)
-
-    def relay_second(i, k):
+            came_right(i, k, p)
+
+            @pl.when(c == 0)
+            def _():
+                going_right(i, k, p, x.at[i, k, p], x.at[i, k, p]).start()
+
+            @pl.when(c == 1)
+            def _():
+                x[i, k, p] = (in_right[par, k, p].astype(f32) + term[k, p]).astype(bf16)
+                going_right(i, k, p, x.at[i, k, p], x.at[i, k, p]).start()
+                going_left(i, k, p, x.at[i, k, p], x.at[i, k, p]).start()
+
+            @pl.when(c >= 2)
+            def _():
+                out[par, k, p] = (in_right[par, k, p].astype(f32) + term[k, p]).astype(bf16)
+                going_right(i, k, p, out.at[par, k, p], in_right.at[par, k, p]).start()
+
+        @pl.when(jnp.logical_and(row == 2, c == 3))
+        def _():
+            came_left(i, k, p)
+            out[par, k, p] = (in_left[par, k, p].astype(f32) + term[k, p]).astype(bf16)
+            going_left(i, k, p, out.at[par, k, p], in_left.at[par, k, p]).start()
+
+    def relay_second(i, k, p, c):
         par = i % 2
 
-        @pl.when(jnp.logical_and(row == 1, side == 1))
-        def _():
-            def body(p, c):
-                came_left(i, k, p)
-                x[i, k, p] = (out[par, k, p].astype(f32) + in_left[par, k, p].astype(f32)).astype(bf16)
-                going_left(i, k, p, x.at[i, k, p], x.at[i, k, p]).start()
-
-            each(body)
+        @pl.when(jnp.logical_and(row == 1, c >= 2))
+        def _():
+            came_left(i, k, p)
+            x[i, k, p] = (out[par, k, p].astype(f32) + in_left[par, k, p].astype(f32)).astype(bf16)
+            going_left(i, k, p, x.at[i, k, p], x.at[i, k, p]).start()
 
         @pl.when(row == 2)
         def _():
-            def body(p, c):
-                came_right(i, k, p)
-
-                @pl.when(c >= 2)
-                def _():
-                    x[i, k, p] = (out[par, k, p].astype(f32) + in_right[par, k, p].astype(f32)).astype(bf16)
-
-                going_right(i, k, p, x.at[i, k, p], x.at[i, k, p]).start()
-
-            each(body)
+            came_right(i, k, p)
+
+            @pl.when(c >= 2)
+            def _():
+                x[i, k, p] = (out[par, k, p].astype(f32) + in_right[par, k, p].astype(f32)).astype(bf16)
+
+            going_right(i, k, p, x.at[i, k, p], x.at[i, k, p]).start()
 
     def came_last(i, k, p, c):
         @pl.when(jnp.logical_and(row == 0, c >= 1))
@@ -266,7 +281,7 @@
             def _():
                 going_left(i, k, p, out.at[0, k, p], in_left.at[0, k, p]).wait_send()
 
-        each(body)
+        each(body, 0, order(i))
 
     def collect(i, k):
         par = i % 2
@@ -286,7 +301,7 @@
                 def _():
                     going_right(i, k, p, in_right.at[par, k, p], in_right.at[par, k, p]).start()
 
-            each(body)
+            each(body, 0, order(i))
 
         @pl.when(row > goal)
         def _():
@@ -297,7 +312,7 @@
                     out[par, k, p] = (in_left[par, k, p].astype(f32) + term[k, p]).astype(bf16)
                     going_left(i, k, p, out.at[par, k, p], in_left.at[par, k, p]).start()
 
-            each(body)
+            each(body, 0, order(i))
 
     def keep(i, k):
         par = i % 2
@@ -330,7 +345,15 @@
 
                     x[i, k, p] = term[k, p].astype(bf16)
 
-            each(body)
+                @pl.when(p // 2 == core)
+                def _():
+                    keep_copy(i, lax.rem(p, 2)).start()
+
+                @pl.when(p // 2 != core)
+                def _():
+                    give_copy(i, lax.rem(p, 2)).start()
+
+            each(body, 0, order(i))
 
     def far_copy(i, k, h):
         return remote(far_out.at[i - 1, k, h], far_in.at[i - 1, k, h], far_send.at[i - 1, k, h], far_recv.at[i - 1, k, h], far)
@@ -339,7 +362,7 @@
         at = pair_index(i, i - 1)
         loaded("f", at)
         if i > 1:
-            partial[k] = ahead[k * width : (k + 1) * width, :]
+            partial[k] = ahead[i - 2, k * width : (k + 1) * width, :]
         else:
             partial[k] = jnp.zeros_like(partial[k])
 
@@ -347,45 +370,64 @@
             came_last(i - 1, k, p, c)
             partial[k] += dot_t(x[i - 1, k, p], factor[at % factor_slots, p // 2, :, span(p)])
 
-        each(body)
+        each(body, 0, order(i - 1))
         for h in range(2):
             far_out[i - 1, k, h] = partial[k, :, h * (rows // 2) : (h + 1) * (rows // 2)].astype(bf16)
             far_copy(i, k, h).start()
-        sent(i - 1, k)
-
-    def look_ahead(i):
-        for j in range(i - 1):
-            at = pair_index(i, j)
-            loaded("f", at)
-
-            def body(p, c):
-                value = dot_t(x[j, :, p].reshape(CHAINS * width, piece), factor[at % factor_slots, p // 2, :, span(p)])
-                if j == 0:
-                    @pl.when(p == 0)
-                    def _():
-                        ahead[...] = value
-
-                    @pl.when(p > 0)
-                    def _():
-                        ahead[...] += value
-                else:
-                    ahead[...] += value
-
-            each(body)
+
+    begun = set()
+
+    def look_ahead(i, j, par, h):
+        at = pair_index(i, j)
+        loaded("f", at)
+        known = [x[j, :, 2 * par + q].reshape(CHAINS * width, piece) for q in range(2)]
+        cols = slice(h * piece, (h + 1) * piece)
+        value = dot_t(jnp.concatenate(known, axis=1), factor[at % factor_slots, par, cols, :])
+        if (i, h) in begun:
+            value = value + ahead[i - 2, :, cols]
+        begun.add((i, h))
+        ahead[i - 2, :, cols] = value
+
+    waiting = [(i, j, par, h) for i in range(2, steps) for j in range(i - 1) for par in range(2) for h in range(2)]
+
+    def take(units):
+        for unit in units:
+            waiting.remove(unit)
+        return units
+
+    def look_due(i):
+        return take([u for u in waiting if u[0] == i + 1])
+
+    def look_more(i):
+        return take([u for u in waiting if u[0] > i + 1 and u[1] < i][:MORE])
+
+    def relay(i, k, units):
+        units = list(units)
+        for stage in (relay_first, relay_second):
+            for q in range(PIECES):
+                p = lax.rem(q + order(i), PIECES)
+                stage(i, k, p, 2 * side + p // 2)
+                if units:
+                    look_ahead(*units.pop(0))
+        for unit in units:
+            look_ahead(*unit)
 
     owner = core == row // 2
     chain_at = lax.rem(row, 2)
 
     def give_copy(i, h):
-        return remote(x.at[i, chain_at, 2 * (1 - core) + h], solved.at[i, h], give_send.at[i, h], give_recv.at[i, h], sibling)
+        p = 2 * (1 - core) + h
+        return remote(x.at[i, chain_at, p], solved.at[i, :, span(h)], give_send.at[i, h], give_recv.at[i, h], sibling)
+
+    def keep_copy(i, h):
+        return pltpu.make_async_copy(x.at[i, chain_at, 2 * core + h], solved.at[i, :, span(h)], keep_sem.at[i, h])
 
     def give(i):
         @pl.when(owner)
         def _():
             for h in range(2):
                 give_copy(i, h).start()
-            for h in range(2):
-                solved[i, h] = x[i, chain_at, 2 * core + h]
+                keep_copy(i, h).start()
 
     def allow(n):
         pl.semaphore_signal(credit.at[n], inc=1, device_id=sibling, device_id_type=MESH)
@@ -394,6 +436,33 @@
         pl.semaphore_wait(credit.at[n], 1)
         local_tile(kind, at).start()
         pushed_tile(kind, at).start()
+
+    def settle_gives(which):
+        @pl.when(owner)
+        def _():
+            for i in which:
+                for h in range(2):
+                    give_copy(i, h).wait_send()
+                    keep_copy(i, h).wait()
+
+        @pl.when(jnp.logical_not(owner))
+        def _():
+            for i in which:
+                for h in range(2):
+                    give_copy(i, h).wait_recv()
+
+    def settle():
+        settle_gives(range(last))
+        for k in range(CHAINS):
+            sent(last - 1, k)
+        for i in range(1, steps):
+            for k in range(CHAINS):
+                for h in range(2):
+                    far_copy(i, k, h).wait_send()
+        for h in range(2):
+            first_push(h, core).wait_send()
+        for kind, at in tiles[1:]:
+            pushed_tile(kind, at).wait_send()
 
     a, b = 0, 1
     turn(0)
@@ -401,14 +470,12 @@
     solve(0, b)
     allow(0)
     turn(1)
-    relay_first(0, a)
-    relay_second(0, a)
+    relay(0, a, [])
     update(1, a)
     refill(0, "i", 3)
     for kind, at in late:
         pushed_tile(kind, at).start()
-    relay_first(0, b)
-    relay_second(0, b)
+    relay(0, b, [])
     for i in range(1, steps):
         solve(i, a)
         update(i, b)
@@ -416,47 +483,27 @@
         if i == 1:
             allow(1)
         if i < last:
-            relay_first(i, a)
-            relay_second(i, a)
+            relay(i, a, look_due(i))
             solve(i, b)
             if i == 1:
                 allow(2)
             turn(i + 1)
-            look_ahead(i + 1)
             update(i + 1, a)
             if i == 1:
                 refill(1, "f", factor_slots)
                 refill(2, "i", 4)
-            relay_first(i, b)
-            relay_second(i, b)
+            relay(i, b, look_more(i))
         else:
             collect(i, a)
             solve(i, b)
             collect(i, b)
+            settle()
             keep(i, a)
             keep(i, b)
-            give(i)
-            sent(i, a)
-            sent(i, b)
-
-    @pl.when(owner)
-    def _():
-        for i in range(steps):
-            for h in range(2):
-                give_copy(i, h).wait_send()
-
-    @pl.when(jnp.logical_not(owner))
-    def _():
-        for i in range(steps):
-            for h in range(2):
-                give_copy(i, h).wait_recv()
-
-    for i in range(1, steps):
-        for k in range(CHAINS):
-            for h in range(2):
-                far_copy(i, k, h).wait_send()
-    for kind, at in tiles:
-        pushed_tile(kind, at).wait_send()
+
+    settle_gives([last])
+    for k in range(CHAINS):
+        sent(last, k)
 
 
 def line_solve(factor_blocks, inverse_blocks, right_sides):
@@ -471,9 +518,9 @@
     dma = pltpu.SemaphoreType.DMA
     solved = pl.pallas_call(
         kernel,
-        out_shape=jax.ShapeDtypeStruct((steps, 2, width, piece), bf16),
+        out_shape=jax.ShapeDtypeStruct((steps, width, col_rows), bf16),
         in_specs=[pl.BlockSpec(memory_space=pl.ANY)] * 3,
-        out_specs=pl.BlockSpec(memory_space=pltpu.VMEM),
+        out_specs=pl.BlockSpec(memory_space=pl.ANY),
         scratch_shapes=[
             pltpu.VMEM((pairs - 1, 2) + factor_blocks.shape[1:], bf16),
             pltpu.VMEM((INVERSE_SLOTS, 2) + inverse_blocks.shape[1:], bf16),
@@ -485,7 +532,7 @@
             pltpu.VMEM(line, bf16),
             pltpu.VMEM((CHAINS, PIECES, width, piece), f32),
             pltpu.VMEM((CHAINS, width, rows), f32),
-            pltpu.VMEM((both, rows), f32),
+            pltpu.VMEM((steps - 2, both, rows), f32),
             pltpu.VMEM((steps - 1, CHAINS, 2, width, half), bf16),
             pltpu.VMEM((steps - 1, CHAINS, 2, width, half), bf16),
             pltpu.VMEM((CHAINS, width, rows), bf16),
@@ -498,13 +545,15 @@
             dma((steps, CHAINS, 2, PIECES)),
             dma((steps, 2)),
             dma((steps, 2)),
+            dma((steps, 2)),
+            dma((3, 2)),
             pltpu.SemaphoreType.REGULAR((3,)),
         ],
         compiler_params=pltpu.CompilerParams(
             collective_id=0, has_side_effects=True, vmem_limit_bytes=67043328
         ),
     )(factor_blocks, inverse_blocks, right_sides)
-    return solved.transpose(0, 1, 3, 2).reshape(steps, col_rows, width)
+    return solved.transpose(0, 2, 1)
 
 
 def plain_solve(factor_blocks, inverse_blocks, right_sides):

time: 113 us -> 101 us (0.89)
  Pallas kernels: 111 us -> 98.7 us
    pallas_call x1, Pallas kernels: 111 us -> 98.7 us  [line_solve(): pl.pallas_call(kernel, out_shape=jax.ShapeDtypeStruct((steps, width, col_...]
    reshape x1 -> x0, local copies, waits for them, and re-layouts: 2.01 us -> none  [line_solve(): return solved.transpose(0, 1, 3, 2).reshape(steps, col_rows, width)]
    unnamed x0 -> x1, local copies, waits for them, and re-layouts: none -> 1.99 us
where the time goes in v2:
time: 101 us
  Pallas kernels  98.7 us (98%)
  local copies, waits for them, and re-layouts  1.99 us (2%)
    pallas_call x1, Pallas kernels, line_solve(): pl.pallas_call(kernel, out_shape=jax.ShapeDtypeStruct((steps, width, col_...  98.7 us

profile of v2, /device:TPU:2, one launch (start us, length us, event | category | flops | bytes accessed | tf_op | source)
XLA Modules:
  0.0 100.7 jit_solution(15585701559233555120)
XLA Ops:
  0.0 98.7 %shard_map.37 = bf16[5,64,1024]{2,1,0:T(8,128)(2,1)} custom-call(bf16[10,1024,1024]{2,1,0:T(8,128)(2,1)} %factor_hbm.1, bf16[5,1024,1024]{2,1,0:T(8,128)(2,1)} %inverse_hbm.1, bf16[5,1024,256]{2,1,0:T(8,128)(2,1)} %right_hbm.1), custom_call_target="tpu_custom_call" | custom-call | tf_op jit(solution)/shard_map/pallas_call | solution.py:519
  98.7 2.0 %copy.5 = bf16[5,1024,64]{1,2,0:T(8,128)(2,1)} copy(bf16[5,1024,64]{1,2,0:T(8,128)(2,1)} %bitcast.1) | data formatting | bytes 1310720

commit v3 on v2

--- a/solution.py
+++ b/solution.py
@@ -132,10 +132,10 @@
         turned[i] = right[i].T
 
     def going_right(i, k, p, src, dst):
-        return remote(src, dst, line_send.at[i, k, 0, p], line_recv.at[i, k, 0, p], right_dev)
+        return remote(src, dst, line_send.at[i % 2, k, 0, p], line_recv.at[i % 2, k, 0, p], right_dev)
 
     def going_left(i, k, p, src, dst):
-        return remote(src, dst, line_send.at[i, k, 1, p], line_recv.at[i, k, 1, p], left)
+        return remote(src, dst, line_send.at[i % 2, k, 1, p], line_recv.at[i % 2, k, 1, p], left)
 
     def each(body, start=0, turned_by=0):
         def step(p, carry):
@@ -356,7 +356,7 @@
             each(body, 0, order(i))
 
     def far_copy(i, k, h):
-        return remote(far_out.at[i - 1, k, h], far_in.at[i - 1, k, h], far_send.at[i - 1, k, h], far_recv.at[i - 1, k, h], far)
+        return remote(far_out.at[i - 1, k, h], far_in.at[i - 1, k, h], far_send.at[i % 2, k, h], far_recv.at[i % 2, k, h], far)
 
     def update(i, k):
         at = pair_index(i, i - 1)
@@ -372,6 +372,8 @@
 
         each(body, 0, order(i - 1))
         for h in range(2):
+            if i > 2:
+                far_copy(i - 2, k, h).wait_send()
             far_out[i - 1, k, h] = partial[k, :, h * (rows // 2) : (h + 1) * (rows // 2)].astype(bf16)
             far_copy(i, k, h).start()
 
@@ -455,7 +457,7 @@
         settle_gives(range(last))
         for k in range(CHAINS):
             sent(last - 1, k)
-        for i in range(1, steps):
+        for i in range(steps - 2, steps):
             for k in range(CHAINS):
                 for h in range(2):
                     far_copy(i, k, h).wait_send()
@@ -539,10 +541,10 @@
             dma((pairs + 2 * steps,)),
             dma((pairs + steps,)),
             dma((pairs + steps,)),
-            dma((steps - 1, CHAINS, 2)),
-            dma((steps - 1, CHAINS, 2)),
-            dma((steps, CHAINS, 2, PIECES)),
-            dma((steps, CHAINS, 2, PIECES)),
+            dma((2, CHAINS, 2)),
+            dma((2, CHAINS, 2)),
+            dma((2, CHAINS, 2, PIECES)),
+            dma((2, CHAINS, 2, PIECES)),
             dma((steps, 2)),
             dma((steps, 2)),
             dma((steps, 2)),

time: 101 us -> 99.8 us (0.988)
  no operation moved by 1% of the time
where the time goes in v3:
time: 99.8 us; the launch traced here: 99.7 us
  Pallas kernels  97.7 us (98%)
  local copies, waits for them, and re-layouts  1.99 us (2%)
    pallas_call x1, Pallas kernels, line_solve(): pl.pallas_call(kernel, out_shape=jax.ShapeDtypeStruct((steps, width, col_...  97.7 us

profile of v3, /device:TPU:2, one launch (start us, length us, event | category | flops | bytes accessed | tf_op | source)
XLA Modules:
  0.0 99.7 jit_solution(3499777878528592143)
XLA Ops:
  0.0 97.7 %shard_map.37 = bf16[5,64,1024]{2,1,0:T(8,128)(2,1)} custom-call(bf16[10,1024,1024]{2,1,0:T(8,128)(2,1)} %factor_hbm.1, bf16[5,1024,1024]{2,1,0:T(8,128)(2,1)} %inverse_hbm.1, bf16[5,1024,256]{2,1,0:T(8,128)(2,1)} %right_hbm.1), custom_call_target="tpu_custom_call" | custom-call | tf_op jit(solution)/shard_map/pallas_call | solution.py:521
  97.7 2.0 %copy.5 = bf16[5,1024,64]{1,2,0:T(8,128)(2,1)} copy(bf16[5,1024,64]{1,2,0:T(8,128)(2,1)} %bitcast.1) | data formatting | bytes 1310720

commit v4 on v3

--- a/solution.py
+++ b/solution.py
@@ -58,16 +58,16 @@
     def pushed_tile(kind, at):
         if kind == "f":
             dst = factor.at[at % factor_slots, core]
-            return remote(factor_hbm.at[at], dst, push_send.at[at], push_recv.at[at], sibling)
+            return remote(factor_hbm.at[at], dst, push_send.at[0], push_recv.at[at], sibling)
         dst = inverse.at[at % INVERSE_SLOTS, core]
-        return remote(inverse_hbm.at[at], dst, push_send.at[pairs + at], push_recv.at[pairs + at], sibling)
+        return remote(inverse_hbm.at[at], dst, push_send.at[1], push_recv.at[pairs + at], sibling)
 
     def landed_tile(kind, at):
         if kind == "f":
             dst = factor.at[at % factor_slots, 1 - core]
-            return remote(factor_hbm.at[at], dst, push_send.at[at], push_recv.at[at], sibling)
+            return remote(factor_hbm.at[at], dst, push_send.at[0], push_recv.at[at], sibling)
         dst = inverse.at[at % INVERSE_SLOTS, 1 - core]
-        return remote(inverse_hbm.at[at], dst, push_send.at[pairs + at], push_recv.at[pairs + at], sibling)
+        return remote(inverse_hbm.at[at], dst, push_send.at[1], push_recv.at[pairs + at], sibling)
 
     tiles = [("i", 0)]
     for i in range(1, steps):
@@ -132,10 +132,10 @@
         turned[i] = right[i].T
 
     def going_right(i, k, p, src, dst):
-        return remote(src, dst, line_send.at[i % 2, k, 0, p], line_recv.at[i % 2, k, 0, p], right_dev)
+        return remote(src, dst, line_send.at[i % 2, k, 0], line_recv.at[i % 2, k, 0, p], right_dev)
 
     def going_left(i, k, p, src, dst):
-        return remote(src, dst, line_send.at[i % 2, k, 1, p], line_recv.at[i % 2, k, 1, p], left)
+        return remote(src, dst, line_send.at[i % 2, k, 1], line_recv.at[i % 2, k, 1, p], left)
 
     def each(body, start=0, turned_by=0):
         def step(p, carry):
@@ -271,17 +271,23 @@
         goal = 2 * core + k
         to_right = row < 3 if i < last else row < goal
         to_left = row > 0 if i < last else row > goal
-
-        def body(p, c):
-            @pl.when(to_right)
-            def _():
-                going_right(i, k, p, out.at[0, k, p], in_right.at[0, k, p]).wait_send()
-
-            @pl.when(jnp.logical_and(to_left, c >= row))
-            def _():
-                going_left(i, k, p, out.at[0, k, p], in_left.at[0, k, p]).wait_send()
-
-        each(body, 0, order(i))
+        most = 2 * side >= row
+
+        def wait(way, pieces):
+            ref = out.at[0, k, pl.ds(0, pieces)]
+            remote(ref, ref, line_send.at[i % 2, k, way], line_recv.at[0, k, way, 0], sibling).wait_send()
+
+        @pl.when(to_right)
+        def _():
+            wait(0, PIECES)
+
+        @pl.when(jnp.logical_and(to_left, most))
+        def _():
+            wait(1, PIECES)
+
+        @pl.when(jnp.logical_and(to_left, jnp.logical_and(jnp.logical_not(most), 2 * side + 1 >= row)))
+        def _():
+            wait(1, PIECES // 2)
 
     def collect(i, k):
         par = i % 2
@@ -419,10 +425,10 @@
 
     def give_copy(i, h):
         p = 2 * (1 - core) + h
-        return remote(x.at[i, chain_at, p], solved.at[i, :, span(h)], give_send.at[i, h], give_recv.at[i, h], sibling)
+        return remote(x.at[i, chain_at, p], solved.at[i, :, span(h)], give_send.at[i // last], give_recv.at[i // last], sibling)
 
     def keep_copy(i, h):
-        return pltpu.make_async_copy(x.at[i, chain_at, 2 * core + h], solved.at[i, :, span(h)], keep_sem.at[i, h])
+        return pltpu.make_async_copy(x.at[i, chain_at, 2 * core + h], solved.at[i, :, span(h)], keep_sem.at[i // last])
 
     def give(i):
         @pl.when(owner)
@@ -439,22 +445,21 @@
         local_tile(kind, at).start()
         pushed_tile(kind, at).start()
 
-    def settle_gives(which):
+    def settle_gives(n):
+        ref = x.at[pl.ds(n * last, 1 if n else last), 0, pl.ds(0, 2)]
+        gift = remote(ref, ref, give_send.at[n], give_recv.at[n], sibling)
+
         @pl.when(owner)
         def _():
-            for i in which:
-                for h in range(2):
-                    give_copy(i, h).wait_send()
-                    keep_copy(i, h).wait()
+            gift.wait_send()
+            pltpu.make_async_copy(ref, ref, keep_sem.at[n]).wait()
 
         @pl.when(jnp.logical_not(owner))
         def _():
-            for i in which:
-                for h in range(2):
-                    give_copy(i, h).wait_recv()
+            gift.wait_recv()
 
     def settle():
-        settle_gives(range(last))
+        settle_gives(0)
         for k in range(CHAINS):
             sent(last - 1, k)
         for i in range(steps - 2, steps):
@@ -463,8 +468,8 @@
                     far_copy(i, k, h).wait_send()
         for h in range(2):
             first_push(h, core).wait_send()
-        for kind, at in tiles[1:]:
-            pushed_tile(kind, at).wait_send()
+        for kind, ref in enumerate((factor_hbm, inverse_hbm.at[pl.ds(1, steps - 1)])):
+            remote(ref, ref, push_send.at[kind], push_recv.at[kind], sibling).wait_send()
 
     a, b = 0, 1
     turn(0)
@@ -503,7 +508,7 @@
             keep(i, a)
             keep(i, b)
 
-    settle_gives([last])
+    settle_gives(1)
     for k in range(CHAINS):
         sent(last, k)
 
@@ -539,15 +544,15 @@
             pltpu.VMEM((steps - 1, CHAINS, 2, width, half), bf16),
             pltpu.VMEM((CHAINS, width, rows), bf16),
             dma((pairs + 2 * steps,)),
-            dma((pairs + steps,)),
+            dma((2,)),
             dma((pairs + steps,)),
             dma((2, CHAINS, 2)),
             dma((2, CHAINS, 2)),
+            dma((2, CHAINS, 2)),
             dma((2, CHAINS, 2, PIECES)),
-            dma((2, CHAINS, 2, PIECES)),
-            dma((steps, 2)),
-            dma((steps, 2)),
-            dma((steps, 2)),
+            dma((2,)),
+            dma((2,)),
+            dma((2,)),
             dma((3, 2)),
             pltpu.SemaphoreType.REGULAR((3,)),
         ],

time: 99.8 us -> 99 us (level)
  no operation moved by 1% of the time
where the time goes in v4:
time: 99 us; the launch traced here: 98.8 us
  Pallas kernels  96.8 us (98%)
  local copies, waits for them, and re-layouts  1.99 us (2%)
    pallas_call x1, Pallas kernels, line_solve(): pl.pallas_call(kernel, out_shape=jax.ShapeDtypeStruct((steps, width, col_...  96.8 us
    unnamed x1, local copies, waits for them, and re-layouts  1.99 us

profile of v4, /device:TPU:2, one launch (start us, length us, event | category | flops | bytes accessed | tf_op | source)
XLA Modules:
  0.0 98.8 jit_solution(4055116567668611607)
XLA Ops:
  0.0 96.8 %shard_map.37 = bf16[5,64,1024]{2,1,0:T(8,128)(2,1)} custom-call(bf16[10,1024,1024]{2,1,0:T(8,128)(2,1)} %factor_hbm.1, bf16[5,1024,1024]{2,1,0:T(8,128)(2,1)} %inverse_hbm.1, bf16[5,1024,256]{2,1,0:T(8,128)(2,1)} %right_hbm.1), custom_call_target="tpu_custom_call" | custom-call | tf_op jit(solution)/shard_map/pallas_call | solution.py:526
  96.8 2.0 %copy.5 = bf16[5,1024,64]{1,2,0:T(8,128)(2,1)} copy(bf16[5,1024,64]{1,2,0:T(8,128)(2,1)} %bitcast.1) | data formatting | bytes 1310720
